TPU v7x, 32 devices: a whole 2x2x4 slice. The times are simulated.
32 devices in a mesh: query: 8 (over z, y), item: 4 (over x, core).
Axes of the slice: x: 2, y: 2, z: 4, core: 2. Of those that a mesh axis runs over, the one named last changes fastest.
Arguments:
- query_emb: bfloat16 [2048, 256], P(('query', 'item')), may hold values from -400 to 400
- targets: int32 [2048], P('query'), may hold values from 0 to 8191, as said below
- eligible_tiles: int32 [32, 32], P('query', 'item'), may hold values from 0 to 1, as said below
- item_feats: bfloat16 [4, 2048, 512], P('item', 'query'), may hold values from -6 to 6
- w_first: bfloat16 [512, 1024], replicated, may hold values from -0.25 to 0.25
- w_second: bfloat16 [1024, 256], replicated, may hold values from -0.1875 to 0.1875
Outputs:
- loss: float32 [2048], P(('query', 'item'))
- query_grad: float32 [2048, 256], P(('query', 'item'))
- w_first_grad: float32 [512, 1024], replicated
- w_second_grad: float32 [1024, 256], replicated
Inputs may be any that keep to these rules, and one draw needn't show every extreme that they name: `eligible_tiles`: every row has at least one 1. The block targets[q] // 256 is marked 1 in row q // 64 of eligible_tiles.
All inputs are finite; a program needn't handle non-finite values.
Results may differ from a plain program's by a relative error of at most 0.007.
Values may be sent and summed in bfloat16 or wider, within the bound.
A program may use at most 64 MiB of HBM per device.

v0:
```python
import math
import jax
import jax.numpy as jnp
from jax import lax
from jax.sharding import PartitionSpec as P


def passed_along(x, axis, by):
    count = lax.axis_size(axis)
    return lax.ppermute(x, axis, [(i, (i + by) % count) for i in range(count)])


def expand_blocks(block_flags, per_block):
    widened = jnp.broadcast_to((block_flags > 0)[..., None], block_flags.shape + (per_block,))
    return widened.reshape(block_flags.shape[:-1] + (block_flags.shape[-1] * per_block,))


def tile_scores(queries, item_tile):
    return 0.25 * jnp.einsum("qe,ie->qi", queries, item_tile, preferred_element_type=jnp.float32)


def on_device(query_emb, targets, eligible_tiles, item_feats, w_first, w_second):
    q_rows = query_emb.shape[0]
    item_count = lax.axis_size("item")
    query_count = lax.axis_size("query")
    item_pos = lax.axis_index("item")
    tokens = item_feats.reshape(item_feats.shape[1], item_feats.shape[2])
    block_rows = tokens.shape[0]
    pre_act = jnp.dot(tokens, w_first, preferred_element_type=jnp.float32)
    hidden = jax.nn.silu(pre_act).astype(jnp.bfloat16)
    own_emb = jnp.dot(hidden, w_second, preferred_element_type=jnp.float32).astype(jnp.bfloat16)
    item_tile = lax.all_gather(own_emb, "query", axis=0, tiled=True)
    tile_rows = item_tile.shape[0]
    emb_width = item_tile.shape[1]
    columns = jnp.arange(tile_rows, dtype=jnp.int32)
    first_item = item_pos * tile_rows
    start_cache = jnp.zeros((1, 1, 1), jnp.bfloat16)

    def forward_step(step_idx, carried):
        visitor, run_max, run_sum, positive, seen = carried
        anchor = (item_pos - step_idx) % item_count
        live_cols = expand_blocks(
            lax.dynamic_index_in_dim(eligible_tiles, anchor, 0, keepdims=False), block_rows
        )[None, :]
        wanted = lax.dynamic_slice_in_dim(targets, anchor * q_rows, q_rows, 0) - first_item
        queries = visitor.astype(jnp.bfloat16)
        scores = tile_scores(queries, item_tile)
        masked = jnp.where(live_cols, scores, -1e30)
        new_max = jnp.maximum(run_max, jnp.max(masked, axis=1))
        added = jnp.sum(jnp.where(live_cols, jnp.exp(masked - new_max[:, None]), 0.0), axis=1)
        run_sum = run_sum * jnp.exp(run_max - new_max) + added
        positive = positive + jnp.sum(
            jnp.where(columns[None, :] == wanted[:, None], scores, 0.0), axis=1
        )
        moved = passed_along((visitor, new_max, run_sum, positive), "item", 1)
        return (moved[0], moved[1], moved[2], moved[3], seen)

    start_state = (
        query_emb.astype(jnp.float32),
        jnp.full((q_rows,), -1e30, jnp.float32),
        jnp.zeros((q_rows,), jnp.float32),
        jnp.zeros((q_rows,), jnp.float32),
        start_cache,
    )
    visitor, run_max, run_sum, positive, seen = lax.fori_loop(
        0, item_count, forward_step, start_state
    )
    log_norm = run_max + jnp.log(run_sum)
    loss = log_norm - positive

    def tile_grads(queries, norm_here, step_idx):
        anchor = (item_pos - step_idx) % item_count
        live_cols = expand_blocks(
            lax.dynamic_index_in_dim(eligible_tiles, anchor, 0, keepdims=False), block_rows
        )[None, :]
        wanted = lax.dynamic_slice_in_dim(targets, anchor * q_rows, q_rows, 0) - first_item
        masked = jnp.where(live_cols, tile_scores(queries, item_tile), -1e30)
        softmax_w = jnp.where(live_cols, jnp.exp(masked - norm_here[:, None]), 0.0)
        coeffs = (softmax_w - (columns[None, :] == wanted[:, None]).astype(jnp.float32)).astype(
            jnp.bfloat16
        )
        q_part = 0.25 * jnp.dot(coeffs, item_tile, preferred_element_type=jnp.float32)
        e_part = 0.25 * jnp.einsum("qi,qe->ie", coeffs, queries, preferred_element_type=jnp.float32)
        return (q_part, e_part)

    zero_q = jnp.zeros((q_rows, emb_width), jnp.float32)
    zero_e = jnp.zeros(item_tile.shape, jnp.float32)

    def backward_step(step_idx, carried):
        travel, emb_grad = carried
        visitor, norm_here, q_grads = travel
        q_part, e_part = tile_grads(visitor.astype(jnp.bfloat16), norm_here, step_idx)
        travel = passed_along((visitor, norm_here, q_grads + q_part), "item", 1)
        return (travel, emb_grad + e_part)

    start_back = ((query_emb.astype(jnp.float32), log_norm, zero_q), zero_e)
    travel, emb_grad = lax.fori_loop(0, item_count, backward_step, start_back)
    query_grad = travel[2]
    own_grad = lax.psum_scatter(emb_grad, "query", scatter_dimension=0, tiled=True).astype(
        jnp.bfloat16
    )
    second_term = jnp.einsum("ih,ie->he", hidden, own_grad, preferred_element_type=jnp.float32)
    hid_grad = jnp.einsum("ie,he->ih", own_grad, w_second, preferred_element_type=jnp.float32)
    gate_sig = jax.nn.sigmoid(pre_act)
    pre_grad = (hid_grad * gate_sig * (1.0 + pre_act * (1.0 - gate_sig))).astype(jnp.bfloat16)
    first_term = jnp.einsum("id,ih->dh", tokens, pre_grad, preferred_element_type=jnp.float32)
    tower_sums = lax.psum((first_term, second_term), ("query", "item"))
    grad_scale = 1.0 / math.sqrt(block_rows * query_count * item_count)
    return (loss, query_grad, tower_sums[0] * grad_scale, tower_sums[1] * grad_scale)


def solution(mesh):
    return jax.shard_map(
        on_device,
        mesh=mesh,
        in_specs=(
            P(("query", "item"), None),
            P("query"),
            P("query", "item"),
            P("item", "query", None),
            P(),
            P(),
        ),
        out_specs=(P(("query", "item")), P(("query", "item"), None), P(), P()),
        check_vma=False,
    )
```

profile of v0, /device:TPU:0, one launch (start us, length us, event | category | flops | bytes accessed | tf_op | source)
XLA Modules:
  0.0 334.7 jit_solution(5722697712973858926)
XLA Ops:
  7.2 0.9 copy.45
  8.1 0.3 copy-done
  8.4 1.4 fusion.22
  9.8 1.0 copy-done.2
  10.8 1.1 convolution_convert_fusion
  12.0 42.9 %all-gather.2.cloned.1.call-done = bf16[2048,256]{1,0:T(8,128)(2,1)} async-done(((bf16[256,256]{1,0:T(8,128)(2,1)}), bf16[2048,256]{1,0:T(8,128)(2,1)}) %all-gather.2.cloned.1.call-update) | async-done | bytes 1048592 | tf_op jit(solution)/shard_map/all_gather | solution.py:32
  54.9 26.8 %while.44 = (s32[]{:T(128)}, bf16[64,256]{1,0:T(8,128)(2,1)S(1)}, f32[64]{0:T(128)S(1)}, f32[64]{0:T(128)S(1)}, f32[64]{0:T(128)S(1)}, /*index=5*/s32[]{:T(128)}...) while((s32[]{:T(128)}, bf16[64,256]{1,0:T(8,128)(2,1)S(1)}, ...), condition=%wide.region_4.5_spmd.clone, body=%wide.region_0.4_spmd.clone.sunk | while | flops 68419800 | bytes 2345530 | solution.py:65
  55.1 1.8 select_reduce_fusion.5
  56.9 1.6 collective-permute-start.1
  58.6 0.3 select_reduce_fusion.6
  59.0 0.6 collective-permute-start.3
  59.7 0.3 collective-permute-done.1
  59.9 2.0 collective-permute-done.2
  62.3 1.8 select_reduce_fusion.5
  64.1 0.7 collective-permute-start.1
  64.8 0.3 select_reduce_fusion.6
  65.3 1.5 collective-permute-start.3
  66.8 0.3 collective-permute-done.1
  67.1 1.1 collective-permute-done.2
  68.2 0.2 collective-permute-done.3
  68.5 1.8 select_reduce_fusion.5
  70.3 1.6 collective-permute-start.1
  72.0 0.3 select_reduce_fusion.6
  72.4 0.6 collective-permute-start.3
  73.0 0.3 collective-permute-done.1
  73.3 2.0 collective-permute-done.2
  75.7 1.8 select_reduce_fusion.5
  77.4 0.7 collective-permute-start.1
  78.2 0.3 select_reduce_fusion.6
  78.6 1.5 collective-permute-start.3
  80.2 0.3 collective-permute-done.1
  80.5 1.1 collective-permute-done.2
  81.7 0.5 fusion.29
  82.3 29.5 %while.45 = (s32[]{:T(128)}, bf16[64,256]{1,0:T(8,128)(2,1)S(1)}, f32[64]{0:T(128)S(1)}, f32[64,256]{1,0:T(8,128)S(1)}, f32[2048,256]{1,0:T(8,128)}, /*index=5*/...) while((s32[]{:T(128)}, bf16[64,256]{1,0:T(8,128)(2,1)S(1)}, ...), condition=%wide.region_6.7_spmd.clone, body=%wide.region_5.6_spmd.clone.sunk | while | flops 203980896 | bytes 11938872 | solution.py:97
  82.4 1.6 collective-permute-start.5
  84.1 1.7 fusion.60
  85.8 0.3 fusion.61
  86.2 1.8 fusion.62
  88.0 1.8 collective-permute-done.6
  89.9 0.7 collective-permute-start.5
  90.7 1.7 fusion.60
  92.4 0.3 fusion.61
  92.9 3.4 %fusion.62 = f32[2048,256]{1,0:T(8,128)} fusion(bf16[64,2048]{1,0:T(8,128)(2,1)S(1)} %fusion.60, f32[2048,256]{1,0:T(8,128)} %get-tuple-element.849, pred[]{:T(512)S(6)} %compare.5, bf16[64,256]{1,0:T(8,128)(2,1)S(1)} %copy.32), kind=kOutput, calls=%fused_computation.12.clone.1 | convolution fusion | flops 68681728 | bytes 4489217 | tf_op jit(solution)/shard_map/while/body/eval_jaxpr/qi,qe->ie/dot_general | solution.py:83
  96.2 0.2 collective-permute-done.6
  96.5 1.4 collective-permute-start.4
  97.8 0.2 collective-permute-start.5
  98.3 1.7 fusion.60
  100.0 0.3 fusion.61
  100.3 0.5 collective-permute-start.6
  100.8 3.4 %fusion.62 = f32[2048,256]{1,0:T(8,128)} fusion(bf16[64,2048]{1,0:T(8,128)(2,1)S(1)} %fusion.60, f32[2048,256]{1,0:T(8,128)} %get-tuple-element.849, pred[]{:T(512)S(6)} %compare.5, bf16[64,256]{1,0:T(8,128)(2,1)S(1)} %copy.32), kind=kOutput, calls=%fused_computation.12.clone.1 | convolution fusion | flops 68681728 | bytes 4489217 | tf_op jit(solution)/shard_map/while/body/eval_jaxpr/qi,qe->ie/dot_general | solution.py:83
  104.2 0.3 collective-permute-start.4
  104.5 1.4 collective-permute-start.5
  106.0 1.7 fusion.60
  107.7 0.3 fusion.61
  108.0 0.3 collective-permute-start.6
  108.3 3.4 %fusion.62 = f32[2048,256]{1,0:T(8,128)} fusion(bf16[64,2048]{1,0:T(8,128)(2,1)S(1)} %fusion.60, f32[2048,256]{1,0:T(8,128)} %get-tuple-element.849, pred[]{:T(512)S(6)} %compare.5, bf16[64,256]{1,0:T(8,128)(2,1)S(1)} %copy.32), kind=kOutput, calls=%fused_computation.12.clone.1 | convolution fusion | flops 68681728 | bytes 4489217 | tf_op jit(solution)/shard_map/while/body/eval_jaxpr/qi,qe->ie/dot_general | solution.py:83
  111.8 66.9 %reduce-scatter.2.cloned.1.call-done = f32[256,256]{1,0:T(8,128)} async-done(((f32[2048,256]{1,0:T(8,128)}), f32[256,256]{1,0:T(8,128)}) %reduce-scatter.2.cloned.1.call-update) | async-done | bytes 262160 | tf_op jit(solution)/shard_map/reduce_scatter | solution.py:99
  178.7 3.2 convolution_bitcast_fusion
  181.9 1.5 fusion.24
  183.4 138.1 %all-reduce.3.cloned.1.call-done = (f32[512,1024]{0,1:T(8,128)}, f32[1024,256]{1,0:T(8,128)}) async-done(((f32[512,1024]{0,1:T(8,128)}, f32[1024,256]{1,0:T(8,128)}), (f32[512,1024]{0,1:T(8,128)}, f32[1024,256]{1,0:T(8,128)})) %all-reduce.3.cloned.1.call-update) | async-done | bytes 3145744 | tf_op jit(solution)/shard_map/psum | solution.py:107
  321.6 1.8 broadcast_multiply_fusion
  323.4 1.8 copy.10
  325.2 2.3 broadcast_multiply_fusion.1
  327.5 0.6 copy.46
  (123 shorter events, 3.1 us)
Async XLA Ops:
  7.2 1.2 copy-start
  7.2 3.6 %copy-start.6 = (bf16[1024,256]{1,0:T(8,128)(2,1)S(1)}, bf16[1024,256]{1,0:T(8,128)(2,1)}, u32[]{:S(2)}) copy-start(bf16[1024,256]{1,0:T(8,128)(2,1)} %param.15) | copy-start | bytes 1572868
  7.2 47.7 %all-gather.2.cloned.1.call-start = ((), (), s32[]{:S(2)}) async-start(), calls=%async_computation.1 | async-start | bytes 1179648 | tf_op jit(solution)/shard_map/all_gather | solution.py:32
  9.8 1.0 copy-start.2
  10.8 44.1 %copy-start.5 = (s32[256]{0:T(256)S(1)}, s32[256]{0:T(256)}, u32[]{:S(2)}) copy-start(s32[256]{0:T(256)} %param.11) | copy-start | bytes 3076
  10.8 44.1 %copy-start.8 = (s32[4,8]{1,0:T(4,128)S(1)}, s32[4,8]{1,0:T(4,128)}, u32[]{:S(2)}) copy-start(s32[4,8]{1,0:T(4,128)} %param.12) | copy-start | bytes 388
  11.9 166.8 %reduce-scatter.2.cloned.1.call-start = ((), (), s32[]{:S(2)}) async-start(), calls=%async_computation.2 | async-start | bytes 2359296 | tf_op jit(solution)/shard_map/reduce_scatter | solution.py:99
  54.9 7.2 %collective-permute-start = (bf16[64,256]{1,0:T(8,128)(2,1)S(1)}, bf16[64,256]{1,0:T(8,128)(2,1)S(1)}, u32[]{:S(2)}, u32[]{:S(2)}) collective-permute-start(bf16[64,256]{1,0:T(8,128)(2,1)S(1)} %copy.17), channel_id=1, source_target_pairs={{0,1},{1,2},{2,3},{3,0},{4,5},{5,6},{6,7},{7,4},{8,9},{9,10},{10,1... | collective-permute-start | bytes 98312 | tf_op jit(solution)/shard_map/while/body/eval_jaxpr/ppermute | solution.py:10
  56.9 3.0 collective-permute-start.1
  58.9 3.0 collective-permute-start.2
  59.0 3.1 collective-permute-start.3
  62.1 6.2 %collective-permute-start = (bf16[64,256]{1,0:T(8,128)(2,1)S(1)}, bf16[64,256]{1,0:T(8,128)(2,1)S(1)}, u32[]{:S(2)}, u32[]{:S(2)}) collective-permute-start(bf16[64,256]{1,0:T(8,128)(2,1)S(1)} %copy.17), channel_id=1, source_target_pairs={{0,1},{1,2},{2,3},{3,0},{4,5},{5,6},{6,7},{7,4},{8,9},{9,10},{10,1... | collective-permute-start | bytes 98312 | tf_op jit(solution)/shard_map/while/body/eval_jaxpr/ppermute | solution.py:10
  64.1 3.0 collective-permute-start.1
  65.2 3.0 collective-permute-start.2
  65.3 3.1 collective-permute-start.3
  68.4 7.1 %collective-permute-start = (bf16[64,256]{1,0:T(8,128)(2,1)S(1)}, bf16[64,256]{1,0:T(8,128)(2,1)S(1)}, u32[]{:S(2)}, u32[]{:S(2)}) collective-permute-start(bf16[64,256]{1,0:T(8,128)(2,1)S(1)} %copy.17), channel_id=1, source_target_pairs={{0,1},{1,2},{2,3},{3,0},{4,5},{5,6},{6,7},{7,4},{8,9},{9,10},{10,1... | collective-permute-start | bytes 98312 | tf_op jit(solution)/shard_map/while/body/eval_jaxpr/ppermute | solution.py:10
  70.3 3.0 collective-permute-start.1
  72.3 3.0 collective-permute-start.2
  72.4 3.1 collective-permute-start.3
  75.5 6.2 %collective-permute-start = (bf16[64,256]{1,0:T(8,128)(2,1)S(1)}, bf16[64,256]{1,0:T(8,128)(2,1)S(1)}, u32[]{:S(2)}, u32[]{:S(2)}) collective-permute-start(bf16[64,256]{1,0:T(8,128)(2,1)S(1)} %copy.17), channel_id=1, source_target_pairs={{0,1},{1,2},{2,3},{3,0},{4,5},{5,6},{6,7},{7,4},{8,9},{9,10},{10,1... | collective-permute-start | bytes 98312 | tf_op jit(solution)/shard_map/while/body/eval_jaxpr/ppermute | solution.py:10
  77.4 3.0 collective-permute-start.1
  78.6 3.0 collective-permute-start.2
  78.6 3.1 collective-permute-start.3
  82.3 3.5 %copy-start.1 = (bf16[2048,256]{1,0:T(8,128)(2,1)S(1)}, bf16[2048,256]{1,0:T(8,128)(2,1)}, u32[]{:S(2)}) copy-start(bf16[2048,256]{1,0:T(8,128)(2,1)} %get-tuple-element.868) | copy-start | bytes 3145732 | tf_op jit(solution)/shard_map/while
  82.3 5.8 %collective-permute-start.4 = (bf16[64,256]{1,0:T(8,128)(2,1)S(1)}, bf16[64,256]{1,0:T(8,128)(2,1)S(1)}, u32[]{:S(2)}, u32[]{:S(2)}) collective-permute-start(bf16[64,256]{1,0:T(8,128)(2,1)S(1)} %copy.32), channel_id=1, source_target_pairs={{0,1},{1,2},{2,3},{3,0},{4,5},{5,6},{6,7},{7,4},{8,9},{9,10},{10,1... | collective-permute-start | bytes 98312 | tf_op jit(solution)/shard_map/while/body/eval_jaxpr/ppermute | solution.py:10
  82.4 5.7 %collective-permute-start.5 = (f32[64]{0:T(128)S(1)}, f32[64]{0:T(128)S(1)}, u32[]{:S(2)}, u32[]{:S(2)}) collective-permute-start(f32[64]{0:T(128)S(1)} %copy.33), channel_id=1, source_target_pairs={{0,1},{1,2},{2,3},{3,0},{4,5},{5,6},{6,7},{7,4},{8,9},{9,10},{10,1... | collective-permute-start | bytes 776 | tf_op jit(solution)/shard_map/while/body/eval_jaxpr/ppermute | solution.py:10
  86.1 3.7 %collective-permute-start.6 = (f32[64,256]{1,0:T(8,128)S(1)}, f32[64,256]{1,0:T(8,128)S(1)}, u32[]{:S(2)}, u32[]{:S(2)}) collective-permute-start(f32[64,256]{1,0:T(8,128)S(1)} %fusion.61), channel_id=1, source_target_pairs={{0,1},{1,2},{2,3},{3,0},{4,5},{5,6},{6,7},{7,4},{8,9},{9,10},{10,1... | collective-permute-start | bytes 196616 | tf_op jit(solution)/shard_map/while/body/eval_jaxpr/ppermute | solution.py:10
  89.9 2.6 copy-start.1
  89.9 6.4 %collective-permute-start.4 = (bf16[64,256]{1,0:T(8,128)(2,1)S(1)}, bf16[64,256]{1,0:T(8,128)(2,1)S(1)}, u32[]{:S(2)}, u32[]{:S(2)}) collective-permute-start(bf16[64,256]{1,0:T(8,128)(2,1)S(1)} %copy.32), channel_id=1, source_target_pairs={{0,1},{1,2},{2,3},{3,0},{4,5},{5,6},{6,7},{7,4},{8,9},{9,10},{10,1... | collective-permute-start | bytes 98312 | tf_op jit(solution)/shard_map/while/body/eval_jaxpr/ppermute | solution.py:10
  89.9 6.4 %collective-permute-start.5 = (f32[64]{0:T(128)S(1)}, f32[64]{0:T(128)S(1)}, u32[]{:S(2)}, u32[]{:S(2)}) collective-permute-start(f32[64]{0:T(128)S(1)} %copy.33), channel_id=1, source_target_pairs={{0,1},{1,2},{2,3},{3,0},{4,5},{5,6},{6,7},{7,4},{8,9},{9,10},{10,1... | collective-permute-start | bytes 776 | tf_op jit(solution)/shard_map/while/body/eval_jaxpr/ppermute | solution.py:10
  92.7 3.7 %collective-permute-start.6 = (f32[64,256]{1,0:T(8,128)S(1)}, f32[64,256]{1,0:T(8,128)S(1)}, u32[]{:S(2)}, u32[]{:S(2)}) collective-permute-start(f32[64,256]{1,0:T(8,128)S(1)} %fusion.61), channel_id=1, source_target_pairs={{0,1},{1,2},{2,3},{3,0},{4,5},{5,6},{6,7},{7,4},{8,9},{9,10},{10,1... | collective-permute-start | bytes 196616 | tf_op jit(solution)/shard_map/while/body/eval_jaxpr/ppermute | solution.py:10
  96.5 3.5 %copy-start.1 = (bf16[2048,256]{1,0:T(8,128)(2,1)S(1)}, bf16[2048,256]{1,0:T(8,128)(2,1)}, u32[]{:S(2)}) copy-start(bf16[2048,256]{1,0:T(8,128)(2,1)} %get-tuple-element.868) | copy-start | bytes 3145732 | tf_op jit(solution)/shard_map/while
  96.5 7.7 %collective-permute-start.4 = (bf16[64,256]{1,0:T(8,128)(2,1)S(1)}, bf16[64,256]{1,0:T(8,128)(2,1)S(1)}, u32[]{:S(2)}, u32[]{:S(2)}) collective-permute-start(bf16[64,256]{1,0:T(8,128)(2,1)S(1)} %copy.32), channel_id=1, source_target_pairs={{0,1},{1,2},{2,3},{3,0},{4,5},{5,6},{6,7},{7,4},{8,9},{9,10},{10,1... | collective-permute-start | bytes 98312 | tf_op jit(solution)/shard_map/while/body/eval_jaxpr/ppermute | solution.py:10
  97.8 6.3 %collective-permute-start.5 = (f32[64]{0:T(128)S(1)}, f32[64]{0:T(128)S(1)}, u32[]{:S(2)}, u32[]{:S(2)}) collective-permute-start(f32[64]{0:T(128)S(1)} %copy.33), channel_id=1, source_target_pairs={{0,1},{1,2},{2,3},{3,0},{4,5},{5,6},{6,7},{7,4},{8,9},{9,10},{10,1... | collective-permute-start | bytes 776 | tf_op jit(solution)/shard_map/while/body/eval_jaxpr/ppermute | solution.py:10
  100.3 3.9 %collective-permute-start.6 = (f32[64,256]{1,0:T(8,128)S(1)}, f32[64,256]{1,0:T(8,128)S(1)}, u32[]{:S(2)}, u32[]{:S(2)}) collective-permute-start(f32[64,256]{1,0:T(8,128)S(1)} %fusion.61), channel_id=1, source_target_pairs={{0,1},{1,2},{2,3},{3,0},{4,5},{5,6},{6,7},{7,4},{8,9},{9,10},{10,1... | collective-permute-start | bytes 196616 | tf_op jit(solution)/shard_map/while/body/eval_jaxpr/ppermute | solution.py:10
  104.2 3.5 %copy-start.1 = (bf16[2048,256]{1,0:T(8,128)(2,1)S(1)}, bf16[2048,256]{1,0:T(8,128)(2,1)}, u32[]{:S(2)}) copy-start(bf16[2048,256]{1,0:T(8,128)(2,1)} %get-tuple-element.868) | copy-start | bytes 3145732 | tf_op jit(solution)/shard_map/while
  104.2 7.5 %collective-permute-start.4 = (bf16[64,256]{1,0:T(8,128)(2,1)S(1)}, bf16[64,256]{1,0:T(8,128)(2,1)S(1)}, u32[]{:S(2)}, u32[]{:S(2)}) collective-permute-start(bf16[64,256]{1,0:T(8,128)(2,1)S(1)} %copy.32), channel_id=1, source_target_pairs={{0,1},{1,2},{2,3},{3,0},{4,5},{5,6},{6,7},{7,4},{8,9},{9,10},{10,1... | collective-permute-start | bytes 98312 | tf_op jit(solution)/shard_map/while/body/eval_jaxpr/ppermute | solution.py:10
  104.5 7.2 %collective-permute-start.5 = (f32[64]{0:T(128)S(1)}, f32[64]{0:T(128)S(1)}, u32[]{:S(2)}, u32[]{:S(2)}) collective-permute-start(f32[64]{0:T(128)S(1)} %copy.33), channel_id=1, source_target_pairs={{0,1},{1,2},{2,3},{3,0},{4,5},{5,6},{6,7},{7,4},{8,9},{9,10},{10,1... | collective-permute-start | bytes 776 | tf_op jit(solution)/shard_map/while/body/eval_jaxpr/ppermute | solution.py:10
  108.0 3.7 %collective-permute-start.6 = (f32[64,256]{1,0:T(8,128)S(1)}, f32[64,256]{1,0:T(8,128)S(1)}, u32[]{:S(2)}, u32[]{:S(2)}) collective-permute-start(f32[64,256]{1,0:T(8,128)S(1)} %fusion.61), channel_id=1, source_target_pairs={{0,1},{1,2},{2,3},{3,0},{4,5},{5,6},{6,7},{7,4},{8,9},{9,10},{10,1... | collective-permute-start | bytes 196616 | tf_op jit(solution)/shard_map/while/body/eval_jaxpr/ppermute | solution.py:10
  111.8 66.9 %copy-start.3 = (f32[256,1024]{1,0:T(8,128)S(1)}, f32[256,1024]{1,0:T(8,128)}, u32[]{:S(2)}) copy-start(f32[256,1024]{1,0:T(8,128)} %copy-done.2) | copy-start | bytes 3145732
  111.8 66.9 %copy-start.4 = (bf16[1,256,512]{2,1,0:T(8,128)(2,1)S(1)}, bf16[1,256,512]{2,1,0:T(8,128)(2,1)}, u32[]{:S(2)}) copy-start(bf16[1,256,512]{2,1,0:T(8,128)(2,1)} %param.13) | copy-start | bytes 786436
  111.8 209.8 %all-reduce.3.cloned.1.call-start = ((), (), s32[]{:S(2)}) async-start(), calls=%async_computation.3 | async-start | bytes 6291456 | tf_op jit(solution)/shard_map/psum | solution.py:107
  178.7 3.2 copy-start.7
Sparse Core Ops, SparseCore 0:
  12.0 42.8 all-gather.1
  111.9 66.7 reduce-scatter.1
  184.8 136.6 all-reduce.2
where the time goes:
time: 335 us
  waiting for transfers between devices  258 us (77%)
  matrix products  34.1 us (10%)
  starting transfers between devices  16 us (5%)
  between operations  13.8 us (4%)
  other arithmetic  6.81 us (2%)
  local copies, waits for them, and re-layouts  5.39 us (2%)
    psum x1, waiting for transfers between devices, on_device(): tower_sums = lax.psum((first_term, second_term), ('query', 'item'))  138 us
    reduce_scatter x1, waiting for transfers between devices, on_device(): lax.psum_scatter(emb_grad, 'query', scatter_dimension=0, tiled=True)  66.9 us
    all_gather x1, waiting for transfers between devices, on_device(): item_tile = lax.all_gather(own_emb, 'query', axis=0, tiled=True)  42.9 us
    ppermute x28, starting transfers between devices, passed_along(): return lax.ppermute(x, axis, [(i, (i + by) % count) for i in range(count)])  15.9 us
    dot_general x8, matrix products, tile_scores(): jnp.einsum('qe,ie->qi', queries, item_tile, preferred_element_type=jnp.fl...  13.8 us
    dot_general x4, matrix products, tile_grads(): jnp.einsum('qi,qe->ie', coeffs, queries, preferred_element_type=jnp.float32)  11.9 us
    ppermute x28, waiting for transfers between devices, passed_along(): return lax.ppermute(x, axis, [(i, (i + by) % count) for i in range(count)])  10.1 us
  transfers between devices with their start and end apart: 31, of which 18 were waited for; matrix products, arithmetic and copies ran while one was open for 9% of the time, Pallas kernels for 0%

commit v1 on v0

--- a/solution.py
+++ b/solution.py
@@ -29,7 +29,14 @@
     pre_act = jnp.dot(tokens, w_first, preferred_element_type=jnp.float32)
     hidden = jax.nn.silu(pre_act).astype(jnp.bfloat16)
     own_emb = jnp.dot(hidden, w_second, preferred_element_type=jnp.float32).astype(jnp.bfloat16)
-    item_tile = lax.all_gather(own_emb, "query", axis=0, tiled=True)
+    ring = [own_emb]
+    for hop in range(7):
+        ring.append(lax.ppermute(ring[-1], "query", [(dev, (dev + 1) % 8) for dev in range(8)]))
+    item_tile = jnp.roll(
+        jnp.concatenate(ring[::-1], axis=0),
+        (lax.axis_index("query") + 1) * ring[0].shape[0],
+        axis=0,
+    )
     tile_rows = item_tile.shape[0]
     emb_width = item_tile.shape[1]
     columns = jnp.arange(tile_rows, dtype=jnp.int32)

time: 335 us -> 339 us (1.012)
  matrix products: 34.1 us -> 23.6 us
  waiting for transfers between devices: 258 us -> 267 us
    ppermute x0 -> x7, waiting for transfers between devices: none -> 53.6 us  [on_device(): lax.ppermute(ring[-1], 'query', [(dev, (dev + 1) % 8) for dev in range(8)])]
    all_gather x1 -> x0, waiting for transfers between devices: 42.9 us -> none  [on_device(): item_tile = lax.all_gather(own_emb, 'query', axis=0, tiled=True)]
    dot_general x8, matrix products: 13.8 us -> 4.01 us  [tile_scores(): jnp.einsum('qe,ie->qi', queries, item_tile, preferred_element_type=jnp.fl...]
  transfers between devices with their start and end apart: 31 -> 37, of which waited for: 18 -> 25; matrix products, arithmetic and copies ran while one was open for 9% -> 6% of each run, Pallas kernels for 0% -> 0%
where the time goes in v1:
time: 339 us
  waiting for transfers between devices  267 us (79%)
  matrix products  23.6 us (7%)
  starting transfers between devices  19.2 us (6%)
  between operations  14.3 us (4%)
  other arithmetic  6.91 us (2%)
  local copies, waits for them, and re-layouts  6.82 us (2%)
    psum x1, waiting for transfers between devices, on_device(): tower_sums = lax.psum((first_term, second_term), ('query', 'item'))  138 us
    reduce_scatter x1, waiting for transfers between devices, on_device(): lax.psum_scatter(emb_grad, 'query', scatter_dimension=0, tiled=True)  65.3 us
    ppermute x7, waiting for transfers between devices, on_device(): lax.ppermute(ring[-1], 'query', [(dev, (dev + 1) % 8) for dev in range(8)])  53.6 us
    ppermute x28, starting transfers between devices, passed_along(): return lax.ppermute(x, axis, [(i, (i + by) % count) for i in range(count)])  16.1 us
    dot_general x4, matrix products, tile_grads(): jnp.einsum('qi,qe->ie', coeffs, queries, preferred_element_type=jnp.float32)  11.9 us
    ppermute x28, waiting for transfers between devices, passed_along(): return lax.ppermute(x, axis, [(i, (i + by) % count) for i in range(count)])  10.3 us
  transfers between devices with their start and end apart: 37, of which 25 were waited for; matrix products, arithmetic and copies ran while one was open for 6% of the time, Pallas kernels for 0%

profile of v1, /device:TPU:0, one launch (start us, length us, event | category | flops | bytes accessed | tf_op | source)
XLA Modules:
  0.0 338.6 jit_solution(9566673776664694384)
XLA Ops:
  7.2 0.9 copy.60
  8.1 0.3 copy-done
  8.4 1.4 fusion.22
  9.8 0.4 convolution_convert_fusion
  10.3 0.5 copy-done.4
  10.8 3.0 collective-permute-start.7
  13.8 6.5 %collective-permute-done.7 = bf16[256,256]{1,0:T(8,128)(2,1)S(1)} collective-permute-done((bf16[256,256]{1,0:T(8,128)(2,1)S(1)}, bf16[256,256]{1,0:T(8,128)(2,1)S(1)}, u32[]{:S(2)}, u32[]{:S(2)}) %collective-permute-start.7) | collective-permute-done | bytes 131104 | tf_op jit(solution)/shard_map/ppermute | solution.py:34
  20.3 7.7 %collective-permute-done.8 = bf16[256,256]{1,0:T(8,128)(2,1)S(1)} collective-permute-done((bf16[256,256]{1,0:T(8,128)(2,1)S(1)}, bf16[256,256]{1,0:T(8,128)(2,1)S(1)}, u32[]{:S(2)}, u32[]{:S(2)}) %collective-permute-start.8) | collective-permute-done | bytes 131104 | tf_op jit(solution)/shard_map/ppermute | solution.py:34
  28.0 7.7 %collective-permute-done.9 = bf16[256,256]{1,0:T(8,128)(2,1)S(1)} collective-permute-done((bf16[256,256]{1,0:T(8,128)(2,1)S(1)}, bf16[256,256]{1,0:T(8,128)(2,1)S(1)}, u32[]{:S(2)}, u32[]{:S(2)}) %collective-permute-start.9) | collective-permute-done | bytes 131104 | tf_op jit(solution)/shard_map/ppermute | solution.py:34
  35.6 7.7 %collective-permute-done.10 = bf16[256,256]{1,0:T(8,128)(2,1)S(1)} collective-permute-done((bf16[256,256]{1,0:T(8,128)(2,1)S(1)}, bf16[256,256]{1,0:T(8,128)(2,1)S(1)}, u32[]{:S(2)}, u32[]{:S(2)}) %collective-permute-start.10) | collective-permute-done | bytes 131104 | tf_op jit(solution)/shard_map/ppermute | solution.py:34
  43.3 7.7 %collective-permute-done.11 = bf16[256,256]{1,0:T(8,128)(2,1)S(1)} collective-permute-done((bf16[256,256]{1,0:T(8,128)(2,1)S(1)}, bf16[256,256]{1,0:T(8,128)(2,1)S(1)}, u32[]{:S(2)}, u32[]{:S(2)}) %collective-permute-start.11) | collective-permute-done | bytes 131104 | tf_op jit(solution)/shard_map/ppermute | solution.py:34
  51.0 8.8 %collective-permute-done.12 = bf16[256,256]{1,0:T(8,128)(2,1)S(1)} collective-permute-done((bf16[256,256]{1,0:T(8,128)(2,1)S(1)}, bf16[256,256]{1,0:T(8,128)(2,1)S(1)}, u32[]{:S(2)}, u32[]{:S(2)}) %collective-permute-start.12) | collective-permute-done | bytes 131104 | tf_op jit(solution)/shard_map/ppermute | solution.py:34
  59.8 7.7 %collective-permute-done.13 = bf16[256,256]{1,0:T(8,128)(2,1)S(1)} collective-permute-done((bf16[256,256]{1,0:T(8,128)(2,1)S(1)}, bf16[256,256]{1,0:T(8,128)(2,1)S(1)}, u32[]{:S(2)}, u32[]{:S(2)}) %collective-permute-start.13) | collective-permute-done | bytes 131104 | tf_op jit(solution)/shard_map/ppermute | solution.py:34
  67.9 0.5 copy-done.3
  68.4 21.9 %while.44 = (s32[]{:T(128)}, bf16[64,256]{1,0:T(8,128)(2,1)S(1)}, f32[64]{0:T(128)S(1)}, f32[64]{0:T(128)S(1)}, f32[64]{0:T(128)S(1)}, /*index=5*/s32[]{:T(128)}...) while((s32[]{:T(128)}, bf16[64,256]{1,0:T(8,128)(2,1)S(1)}, ...), condition=%wide.region_4.5_spmd.clone, body=%wide.region_0.4_spmd.clone.sunk | while | flops 68419800 | bytes 2345530 | solution.py:72
  68.6 0.5 select_reduce_fusion.5
  69.1 2.0 collective-permute-start.1
  71.2 0.3 select_reduce_fusion.6
  71.9 0.3 collective-permute-done.1
  72.1 2.4 collective-permute-done.2
  74.8 0.5 select_reduce_fusion.5
  75.4 0.3 collective-permute-start.1
  75.8 0.3 select_reduce_fusion.6
  76.2 1.9 collective-permute-start.3
  78.2 0.3 collective-permute-done.1
  78.4 0.7 collective-permute-done.2
  79.5 0.5 select_reduce_fusion.5
  80.0 2.0 collective-permute-start.1
  82.1 0.3 select_reduce_fusion.6
  83.0 2.4 collective-permute-done.2
  85.8 0.5 select_reduce_fusion.5
  86.3 0.3 collective-permute-start.1
  86.7 0.3 select_reduce_fusion.6
  87.1 1.9 collective-permute-start.3
  89.1 0.3 collective-permute-done.1
  89.3 0.7 collective-permute-done.2
  90.2 0.5 fusion.29
  90.8 24.9 %while.45 = (s32[]{:T(128)}, bf16[64,256]{1,0:T(8,128)(2,1)S(1)}, f32[64]{0:T(128)S(1)}, f32[64,256]{1,0:T(8,128)S(1)}, f32[2048,256]{1,0:T(8,128)}, /*index=5*/...) while((s32[]{:T(128)}, bf16[64,256]{1,0:T(8,128)(2,1)S(1)}, ...), condition=%wide.region_6.7_spmd.clone, body=%wide.region_5.6_spmd.clone.sunk | while | flops 203980896 | bytes 7744540 | solution.py:104
  90.9 1.9 collective-permute-start.5
  93.0 0.5 fusion.60
  93.5 0.3 fusion.61
  93.9 1.8 fusion.62
  95.7 1.8 collective-permute-done.6
  97.5 0.3 collective-permute-start.5
  98.0 0.5 fusion.60
  98.5 0.3 fusion.61
  99.0 3.4 fusion.62
  102.5 1.7 collective-permute-start.4
  104.7 0.5 fusion.60
  105.1 0.3 fusion.61
  105.6 3.4 fusion.62
  109.2 1.7 collective-permute-start.5
  111.2 0.5 fusion.60
  111.6 0.3 fusion.61
  111.9 0.3 collective-permute-start.6
  112.2 3.4 fusion.62
  115.8 65.3 %reduce-scatter.2.cloned.1.call-done = f32[256,256]{1,0:T(8,128)} async-done(((f32[2048,256]{1,0:T(8,128)}), f32[256,256]{1,0:T(8,128)}) %reduce-scatter.2.cloned.1.call-update) | async-done | bytes 262160 | tf_op jit(solution)/shard_map/reduce_scatter | solution.py:106
  181.1 3.2 convolution_bitcast_fusion
  184.3 1.5 fusion.24
  185.8 138.1 %all-reduce.3.cloned.1.call-done = (f32[512,1024]{0,1:T(8,128)}, f32[1024,256]{1,0:T(8,128)}) async-done(((f32[512,1024]{0,1:T(8,128)}, f32[1024,256]{1,0:T(8,128)}), (f32[512,1024]{0,1:T(8,128)}, f32[1024,256]{1,0:T(8,128)})) %all-reduce.3.cloned.1.call-update) | async-done | bytes 3145744 | tf_op jit(solution)/shard_map/psum | solution.py:114
  323.9 3.1 broadcast_multiply_fusion
  327.1 3.0 copy.10
  330.1 1.1 broadcast_multiply_fusion.1
  331.1 0.6 copy.61
  (150 shorter events, 5.1 us)
Async XLA Ops:
  7.2 1.2 copy-start
  7.2 2.6 copy-start.9
  7.2 173.9 %reduce-scatter.2.cloned.1.call-start = ((), (), s32[]{:S(2)}) async-start(), calls=%async_computation.1 | async-start | bytes 2359296 | tf_op jit(solution)/shard_map/reduce_scatter | solution.py:106
  8.4 51.4 %copy-start.1 = (bf16[64,256]{1,0:T(8,128)(2,1)}, bf16[64,256]{1,0:T(8,128)(2,1)S(1)}, u32[]{:S(2)}) copy-start(bf16[64,256]{1,0:T(8,128)(2,1)S(1)} %copy.60) | copy-start | bytes 98308
  9.8 1.0 copy-start.4
  10.8 9.5 %collective-permute-start.7 = (bf16[256,256]{1,0:T(8,128)(2,1)S(1)}, bf16[256,256]{1,0:T(8,128)(2,1)S(1)}, u32[]{:S(2)}, u32[]{:S(2)}) collective-permute-start(bf16[256,256]{1,0:T(8,128)(2,1)S(1)} %convolution_convert_fusion), channel_id=1, source_target_pairs={{0,4},{4,8},{8,12},{12,16},{16,20},{20,24},{24,28},{28,0},{1,5},{5... | collective-permute-start | bytes 393224 | tf_op jit(solution)/shard_map/ppermute | solution.py:34
  20.3 7.7 %collective-permute-start.8 = (bf16[256,256]{1,0:T(8,128)(2,1)S(1)}, bf16[256,256]{1,0:T(8,128)(2,1)S(1)}, u32[]{:S(2)}, u32[]{:S(2)}) collective-permute-start(bf16[256,256]{1,0:T(8,128)(2,1)S(1)} %collective-permute-done.7), channel_id=1, source_target_pairs={{0,4},{4,8},{8,12},{12,16},{16,20},{20,24},{24,28},{28,0},{1,5},{5... | collective-permute-start | bytes 393224 | tf_op jit(solution)/shard_map/ppermute | solution.py:34
  28.0 7.7 %collective-permute-start.9 = (bf16[256,256]{1,0:T(8,128)(2,1)S(1)}, bf16[256,256]{1,0:T(8,128)(2,1)S(1)}, u32[]{:S(2)}, u32[]{:S(2)}) collective-permute-start(bf16[256,256]{1,0:T(8,128)(2,1)S(1)} %collective-permute-done.8), channel_id=1, source_target_pairs={{0,4},{4,8},{8,12},{12,16},{16,20},{20,24},{24,28},{28,0},{1,5},{5... | collective-permute-start | bytes 393224 | tf_op jit(solution)/shard_map/ppermute | solution.py:34
  35.6 7.7 %collective-permute-start.10 = (bf16[256,256]{1,0:T(8,128)(2,1)S(1)}, bf16[256,256]{1,0:T(8,128)(2,1)S(1)}, u32[]{:S(2)}, u32[]{:S(2)}) collective-permute-start(bf16[256,256]{1,0:T(8,128)(2,1)S(1)} %collective-permute-done.9), channel_id=1, source_target_pairs={{0,4},{4,8},{8,12},{12,16},{16,20},{20,24},{24,28},{28,0},{1,5},{5... | collective-permute-start | bytes 393224 | tf_op jit(solution)/shard_map/ppermute | solution.py:34
  43.3 7.7 %collective-permute-start.11 = (bf16[256,256]{1,0:T(8,128)(2,1)S(1)}, bf16[256,256]{1,0:T(8,128)(2,1)S(1)}, u32[]{:S(2)}, u32[]{:S(2)}) collective-permute-start(bf16[256,256]{1,0:T(8,128)(2,1)S(1)} %collective-permute-done.10), channel_id=1, source_target_pairs={{0,4},{4,8},{8,12},{12,16},{16,20},{20,24},{24,28},{28,0},{1,5},{5... | collective-permute-start | bytes 393224 | tf_op jit(solution)/shard_map/ppermute | solution.py:34
  51.0 8.8 %collective-permute-start.12 = (bf16[256,256]{1,0:T(8,128)(2,1)S(1)}, bf16[256,256]{1,0:T(8,128)(2,1)S(1)}, u32[]{:S(2)}, u32[]{:S(2)}) collective-permute-start(bf16[256,256]{1,0:T(8,128)(2,1)S(1)} %collective-permute-done.11), channel_id=1, source_target_pairs={{0,4},{4,8},{8,12},{12,16},{16,20},{20,24},{24,28},{28,0},{1,5},{5... | collective-permute-start | bytes 393224 | tf_op jit(solution)/shard_map/ppermute | solution.py:34
  59.8 7.7 %collective-permute-start.13 = (bf16[256,256]{1,0:T(8,128)(2,1)S(1)}, bf16[256,256]{1,0:T(8,128)(2,1)S(1)}, u32[]{:S(2)}, u32[]{:S(2)}) collective-permute-start(bf16[256,256]{1,0:T(8,128)(2,1)S(1)} %collective-permute-done.12), channel_id=1, source_target_pairs={{0,4},{4,8},{8,12},{12,16},{16,20},{20,24},{24,28},{28,0},{1,5},{5... | collective-permute-start | bytes 393224 | tf_op jit(solution)/shard_map/ppermute | solution.py:34
  67.6 0.8 copy-start.3
  67.6 0.8 copy-start.8
  67.6 0.7 copy-start.11
  68.4 22.4 %copy-start.2 = (bf16[64,256]{1,0:T(8,128)(2,1)S(1)}, bf16[64,256]{1,0:T(8,128)(2,1)}, u32[]{:S(2)}) copy-start(bf16[64,256]{1,0:T(8,128)(2,1)} %copy-done.1) | copy-start | bytes 98308
  68.4 6.3 %collective-permute-start = (bf16[64,256]{1,0:T(8,128)(2,1)S(1)}, bf16[64,256]{1,0:T(8,128)(2,1)S(1)}, u32[]{:S(2)}, u32[]{:S(2)}) collective-permute-start(bf16[64,256]{1,0:T(8,128)(2,1)S(1)} %copy.32), channel_id=1, source_target_pairs={{0,1},{1,2},{2,3},{3,0},{4,5},{5,6},{6,7},{7,4},{8,9},{9,10},{10,1... | collective-permute-start | bytes 98312 | tf_op jit(solution)/shard_map/while/body/eval_jaxpr/ppermute | solution.py:10
  69.1 3.0 collective-permute-start.1
  71.5 3.0 collective-permute-start.2
  71.6 3.1 collective-permute-start.3
  74.7 4.6 %collective-permute-start = (bf16[64,256]{1,0:T(8,128)(2,1)S(1)}, bf16[64,256]{1,0:T(8,128)(2,1)S(1)}, u32[]{:S(2)}, u32[]{:S(2)}) collective-permute-start(bf16[64,256]{1,0:T(8,128)(2,1)S(1)} %copy.32), channel_id=1, source_target_pairs={{0,1},{1,2},{2,3},{3,0},{4,5},{5,6},{6,7},{7,4},{8,9},{9,10},{10,1... | collective-permute-start | bytes 98312 | tf_op jit(solution)/shard_map/while/body/eval_jaxpr/ppermute | solution.py:10
  75.4 3.0 collective-permute-start.1
  76.1 3.0 collective-permute-start.2
  76.2 3.1 collective-permute-start.3
  79.3 6.3 %collective-permute-start = (bf16[64,256]{1,0:T(8,128)(2,1)S(1)}, bf16[64,256]{1,0:T(8,128)(2,1)S(1)}, u32[]{:S(2)}, u32[]{:S(2)}) collective-permute-start(bf16[64,256]{1,0:T(8,128)(2,1)S(1)} %copy.32), channel_id=1, source_target_pairs={{0,1},{1,2},{2,3},{3,0},{4,5},{5,6},{6,7},{7,4},{8,9},{9,10},{10,1... | collective-permute-start | bytes 98312 | tf_op jit(solution)/shard_map/while/body/eval_jaxpr/ppermute | solution.py:10
  80.0 3.0 collective-permute-start.1
  82.4 3.0 collective-permute-start.2
  82.5 3.1 collective-permute-start.3
  85.6 4.6 %collective-permute-start = (bf16[64,256]{1,0:T(8,128)(2,1)S(1)}, bf16[64,256]{1,0:T(8,128)(2,1)S(1)}, u32[]{:S(2)}, u32[]{:S(2)}) collective-permute-start(bf16[64,256]{1,0:T(8,128)(2,1)S(1)} %copy.32), channel_id=1, source_target_pairs={{0,1},{1,2},{2,3},{3,0},{4,5},{5,6},{6,7},{7,4},{8,9},{9,10},{10,1... | collective-permute-start | bytes 98312 | tf_op jit(solution)/shard_map/while/body/eval_jaxpr/ppermute | solution.py:10
  86.3 3.0 collective-permute-start.1
  87.0 3.0 collective-permute-start.2
  87.1 3.1 collective-permute-start.3
  90.8 4.9 %collective-permute-start.4 = (bf16[64,256]{1,0:T(8,128)(2,1)S(1)}, bf16[64,256]{1,0:T(8,128)(2,1)S(1)}, u32[]{:S(2)}, u32[]{:S(2)}) collective-permute-start(bf16[64,256]{1,0:T(8,128)(2,1)S(1)} %copy.47), channel_id=1, source_target_pairs={{0,1},{1,2},{2,3},{3,0},{4,5},{5,6},{6,7},{7,4},{8,9},{9,10},{10,1... | collective-permute-start | bytes 98312 | tf_op jit(solution)/shard_map/while/body/eval_jaxpr/ppermute | solution.py:10
  90.9 4.8 %collective-permute-start.5 = (f32[64]{0:T(128)S(1)}, f32[64]{0:T(128)S(1)}, u32[]{:S(2)}, u32[]{:S(2)}) collective-permute-start(f32[64]{0:T(128)S(1)} %copy.48), channel_id=1, source_target_pairs={{0,1},{1,2},{2,3},{3,0},{4,5},{5,6},{6,7},{7,4},{8,9},{9,10},{10,1... | collective-permute-start | bytes 776 | tf_op jit(solution)/shard_map/while/body/eval_jaxpr/ppermute | solution.py:10
  93.8 3.7 %collective-permute-start.6 = (f32[64,256]{1,0:T(8,128)S(1)}, f32[64,256]{1,0:T(8,128)S(1)}, u32[]{:S(2)}, u32[]{:S(2)}) collective-permute-start(f32[64,256]{1,0:T(8,128)S(1)} %fusion.61), channel_id=1, source_target_pairs={{0,1},{1,2},{2,3},{3,0},{4,5},{5,6},{6,7},{7,4},{8,9},{9,10},{10,1... | collective-permute-start | bytes 196616 | tf_op jit(solution)/shard_map/while/body/eval_jaxpr/ppermute | solution.py:10
  97.5 4.8 %collective-permute-start.4 = (bf16[64,256]{1,0:T(8,128)(2,1)S(1)}, bf16[64,256]{1,0:T(8,128)(2,1)S(1)}, u32[]{:S(2)}, u32[]{:S(2)}) collective-permute-start(bf16[64,256]{1,0:T(8,128)(2,1)S(1)} %copy.47), channel_id=1, source_target_pairs={{0,1},{1,2},{2,3},{3,0},{4,5},{5,6},{6,7},{7,4},{8,9},{9,10},{10,1... | collective-permute-start | bytes 98312 | tf_op jit(solution)/shard_map/while/body/eval_jaxpr/ppermute | solution.py:10
  97.5 4.8 %collective-permute-start.5 = (f32[64]{0:T(128)S(1)}, f32[64]{0:T(128)S(1)}, u32[]{:S(2)}, u32[]{:S(2)}) collective-permute-start(f32[64]{0:T(128)S(1)} %copy.48), channel_id=1, source_target_pairs={{0,1},{1,2},{2,3},{3,0},{4,5},{5,6},{6,7},{7,4},{8,9},{9,10},{10,1... | collective-permute-start | bytes 776 | tf_op jit(solution)/shard_map/while/body/eval_jaxpr/ppermute | solution.py:10
  98.8 3.7 %collective-permute-start.6 = (f32[64,256]{1,0:T(8,128)S(1)}, f32[64,256]{1,0:T(8,128)S(1)}, u32[]{:S(2)}, u32[]{:S(2)}) collective-permute-start(f32[64,256]{1,0:T(8,128)S(1)} %fusion.61), channel_id=1, source_target_pairs={{0,1},{1,2},{2,3},{3,0},{4,5},{5,6},{6,7},{7,4},{8,9},{9,10},{10,1... | collective-permute-start | bytes 196616 | tf_op jit(solution)/shard_map/while/body/eval_jaxpr/ppermute | solution.py:10
  102.5 6.4 %collective-permute-start.4 = (bf16[64,256]{1,0:T(8,128)(2,1)S(1)}, bf16[64,256]{1,0:T(8,128)(2,1)S(1)}, u32[]{:S(2)}, u32[]{:S(2)}) collective-permute-start(bf16[64,256]{1,0:T(8,128)(2,1)S(1)} %copy.47), channel_id=1, source_target_pairs={{0,1},{1,2},{2,3},{3,0},{4,5},{5,6},{6,7},{7,4},{8,9},{9,10},{10,1... | collective-permute-start | bytes 98312 | tf_op jit(solution)/shard_map/while/body/eval_jaxpr/ppermute | solution.py:10
  104.2 4.7 %collective-permute-start.5 = (f32[64]{0:T(128)S(1)}, f32[64]{0:T(128)S(1)}, u32[]{:S(2)}, u32[]{:S(2)}) collective-permute-start(f32[64]{0:T(128)S(1)} %copy.48), channel_id=1, source_target_pairs={{0,1},{1,2},{2,3},{3,0},{4,5},{5,6},{6,7},{7,4},{8,9},{9,10},{10,1... | collective-permute-start | bytes 776 | tf_op jit(solution)/shard_map/while/body/eval_jaxpr/ppermute | solution.py:10
  105.4 3.7 %collective-permute-start.6 = (f32[64,256]{1,0:T(8,128)S(1)}, f32[64,256]{1,0:T(8,128)S(1)}, u32[]{:S(2)}, u32[]{:S(2)}) collective-permute-start(f32[64,256]{1,0:T(8,128)S(1)} %fusion.61), channel_id=1, source_target_pairs={{0,1},{1,2},{2,3},{3,0},{4,5},{5,6},{6,7},{7,4},{8,9},{9,10},{10,1... | collective-permute-start | bytes 196616 | tf_op jit(solution)/shard_map/while/body/eval_jaxpr/ppermute | solution.py:10
  109.2 6.4 %collective-permute-start.4 = (bf16[64,256]{1,0:T(8,128)(2,1)S(1)}, bf16[64,256]{1,0:T(8,128)(2,1)S(1)}, u32[]{:S(2)}, u32[]{:S(2)}) collective-permute-start(bf16[64,256]{1,0:T(8,128)(2,1)S(1)} %copy.47), channel_id=1, source_target_pairs={{0,1},{1,2},{2,3},{3,0},{4,5},{5,6},{6,7},{7,4},{8,9},{9,10},{10,1... | collective-permute-start | bytes 98312 | tf_op jit(solution)/shard_map/while/body/eval_jaxpr/ppermute | solution.py:10
  109.2 6.4 %collective-permute-start.5 = (f32[64]{0:T(128)S(1)}, f32[64]{0:T(128)S(1)}, u32[]{:S(2)}, u32[]{:S(2)}) collective-permute-start(f32[64]{0:T(128)S(1)} %copy.48), channel_id=1, source_target_pairs={{0,1},{1,2},{2,3},{3,0},{4,5},{5,6},{6,7},{7,4},{8,9},{9,10},{10,1... | collective-permute-start | bytes 776 | tf_op jit(solution)/shard_map/while/body/eval_jaxpr/ppermute | solution.py:10
  111.9 3.7 %collective-permute-start.6 = (f32[64,256]{1,0:T(8,128)S(1)}, f32[64,256]{1,0:T(8,128)S(1)}, u32[]{:S(2)}, u32[]{:S(2)}) collective-permute-start(f32[64,256]{1,0:T(8,128)S(1)} %fusion.61), channel_id=1, source_target_pairs={{0,1},{1,2},{2,3},{3,0},{4,5},{5,6},{6,7},{7,4},{8,9},{9,10},{10,1... | collective-permute-start | bytes 196616 | tf_op jit(solution)/shard_map/while/body/eval_jaxpr/ppermute | solution.py:10
  115.7 65.4 %copy-start.5 = (f32[256,1024]{1,0:T(8,128)S(1)}, f32[256,1024]{1,0:T(8,128)}, u32[]{:S(2)}) copy-start(f32[256,1024]{1,0:T(8,128)} %copy-done.4) | copy-start | bytes 3145732
  115.7 65.4 %copy-start.7 = (bf16[1,256,512]{2,1,0:T(8,128)(2,1)S(1)}, bf16[1,256,512]{2,1,0:T(8,128)(2,1)}, u32[]{:S(2)}) copy-start(bf16[1,256,512]{2,1,0:T(8,128)(2,1)} %param.13) | copy-start | bytes 786436
  115.7 208.2 %all-reduce.3.cloned.1.call-start = ((), (), s32[]{:S(2)}) async-start(), calls=%async_computation.2 | async-start | bytes 6291456 | tf_op jit(solution)/shard_map/psum | solution.py:114
  181.1 3.2 copy-start.10
  327.1 3.0 copy-start.6
Sparse Core Ops, SparseCore 0:
  115.8 65.2 reduce-scatter.1
  187.2 136.6 all-reduce.2
